TPU v7x, 32 devices: a whole 2x2x4 slice. The times are simulated.
32 devices in a mesh: batch: 8 (over z, y), head: 4 (over x, core).
Axes of the slice: x: 2, y: 2, z: 4, core: 2. Of those that a mesh axis runs over, the one named last changes fastest.
Arguments:
- tokens: bfloat16 [16384, 768], P(('batch', 'head')), may hold values from -6 to 6
- cotangent: bfloat16 [16384, 768], P(('batch', 'head')), may hold values from -6 to 6
- lengths: int32 [32], P('batch'), may hold values from 16 to 512, as said below
- labels: int32 [32], P('batch'), may hold values from 0 to 2
- w_qkv: bfloat16 [768, 2304], replicated, may hold values from -0.21875 to 0.21875
- w_out: bfloat16 [768, 768], replicated, may hold values from -0.875 to 0.875
- w_up: bfloat16 [768, 3072], replicated, may hold values from -0.21875 to 0.21875
- w_down: bfloat16 [3072, 768], replicated, may hold values from -0.109375 to 0.109375
- w_pool: bfloat16 [768, 768], replicated, may hold values from -0.21875 to 0.21875
- w_class: bfloat16 [3, 768], replicated, may hold values from -0.625 to 0.625
- biases: float32 [7, 768], replicated, may hold values from -3 to 3
- norm_gains: float32 [2, 768], replicated, may hold values from 0.25 to 1.75
- bias_up: float32 [3072], replicated, may hold values from -3 to 3
Outputs:
- out: bfloat16 [16384, 768], P(('batch', 'head'))
- grad_tokens: bfloat16 [16384, 768], P(('batch', 'head'))
- losses: float32 [32], P(('batch', 'head'))
- g_qkv: float32 [768, 2304], P(None, ('batch', 'head'))
- g_out: float32 [768, 768], P(None, ('batch', 'head'))
- g_up: float32 [768, 3072], P(None, ('batch', 'head'))
- g_down: float32 [3072, 768], P(None, ('batch', 'head'))
- g_pool: float32 [768, 768], P(None, ('batch', 'head'))
- g_class: float32 [3, 768], P(None, ('batch', 'head'))
- g_biases: float32 [6, 768], P(None, ('batch', 'head'))
- g_gains: float32 [2, 768], P(None, ('batch', 'head'))
- g_bias_up: float32 [3072], P(('batch', 'head'))
- g_pool_bias: float32 [768], P(('batch', 'head'))
Inputs may be any that keep to these rules, and one draw needn't show every extreme that they name: `lengths`: some sequence has exactly 512 and some exactly 16 positions.
All inputs are finite; a program needn't handle non-finite values.
Results may differ from a plain program's by a relative error of at most 0.014.
Values may be sent and summed in bfloat16 or wider, within the bound.
A program may use at most 192 MiB of HBM per device.

v0:
```python
import jax
import jax.numpy as jnp
from jax import lax
from jax.sharding import PartitionSpec as P

D = 768
HEADS = 12
HEAD_DIM = 64
CLASSES = 3
SLOT = 512


def layer_norm(hidden, gain, shift):
    center = hidden - jnp.mean(hidden, axis=-1, keepdims=True)
    spread = jnp.mean(center * center, axis=-1, keepdims=True)
    return center * lax.rsqrt(spread + 1e-12) * gain + shift


def exact_gelu(hidden):
    return jax.nn.gelu(hidden, approximate=False)


def inner(left, right):
    return lax.dot_general(
        left, right, (((0,), (0,)), ((), ())), preferred_element_type=jnp.float32
    )


def against(left, right):
    return lax.dot_general(
        left, right, (((1,), (1,)), ((), ())), preferred_element_type=jnp.float32
    )


def exact(left, right):
    return jnp.dot(left, right, precision=lax.Precision.HIGHEST, preferred_element_type=jnp.float32)


def masked_scores(queries, keys_all, length):
    scores = jnp.einsum(
        "qhd,khd->hqk", queries, keys_all, preferred_element_type=jnp.float32
    ) * HEAD_DIM ** (-0.5)
    allowed = jnp.arange(SLOT) < length
    return jnp.where(allowed[None, None, :], scores, -1e30)


def attend_forward(seq_item):
    packed, length = seq_item
    queries = packed[:, 0]
    keys_all = packed[:, 1]
    values = packed[:, 2]
    scores = masked_scores(queries, keys_all, length)
    row_max = jnp.max(scores, axis=-1, keepdims=True)
    exp_sum = jnp.sum(jnp.exp(scores - row_max), axis=-1, keepdims=True)
    log_total = row_max + jnp.log(exp_sum)
    weights = jnp.exp(scores - log_total).astype(jnp.bfloat16)
    context = jnp.einsum("hqk,khd->qhd", weights, values, preferred_element_type=jnp.float32)
    return (context.astype(jnp.bfloat16), log_total)


def attend_backward(seq_item):
    packed, log_total, d_context, length = seq_item
    queries = packed[:, 0]
    keys_all = packed[:, 1]
    values = packed[:, 2]
    scores = masked_scores(queries, keys_all, length)
    weights = jnp.exp(scores - log_total)
    weights_low = weights.astype(jnp.bfloat16)
    d_weights = jnp.einsum("qhd,khd->hqk", d_context, values, preferred_element_type=jnp.float32)
    d_values = jnp.einsum(
        "hqk,qhd->khd", weights_low, d_context, preferred_element_type=jnp.float32
    )
    row_dot = jnp.sum(weights * d_weights, axis=-1, keepdims=True)
    d_scores = (weights * (d_weights - row_dot)).astype(jnp.bfloat16)
    d_queries = jnp.einsum(
        "hqk,khd->qhd", d_scores, keys_all, preferred_element_type=jnp.float32
    ) * HEAD_DIM ** (-0.5)
    d_keys = jnp.einsum(
        "hqk,qhd->khd", d_scores, queries, preferred_element_type=jnp.float32
    ) * HEAD_DIM ** (-0.5)
    return jnp.stack([d_queries, d_keys, d_values], axis=1).astype(jnp.bfloat16)


def per_device(
    tokens,
    cotangent,
    lengths,
    labels,
    w_qkv,
    w_out,
    w_up,
    w_down,
    w_pool,
    w_class,
    biases,
    norm_gains,
    bias_up,
):
    head_parts = lax.axis_size("head")
    head_rank = lax.axis_index("head")
    tok_rows = tokens.shape[0]
    own_seqs = tok_rows // SLOT
    local_heads = HEADS // head_parts
    slice_width = D // head_parts
    own_lengths = lax.dynamic_slice_in_dim(lengths, head_rank * own_seqs, own_seqs)
    own_labels = lax.dynamic_slice_in_dim(labels, head_rank * own_seqs, own_seqs)
    slot_live = (
        (jnp.arange(SLOT)[None, :] < own_lengths[:, None]).reshape(tok_rows).astype(jnp.float32)
    )
    zeros_key = jnp.zeros((D,), jnp.float32)
    packed = jnp.dot(tokens, w_qkv, preferred_element_type=jnp.float32) + jnp.concatenate(
        [biases[0], zeros_key, biases[1]]
    )
    packed_low = packed.astype(jnp.bfloat16)
    head_view = lax.all_to_all(
        packed_low.reshape(tok_rows, 3, head_parts, slice_width),
        "head",
        split_axis=2,
        concat_axis=0,
        tiled=True,
    )
    seq_view = head_view.reshape(head_parts * own_seqs, SLOT, 3, local_heads, HEAD_DIM)
    context, log_total = lax.map(attend_forward, (seq_view, lengths))
    context_back = lax.all_to_all(
        context.reshape(head_parts * tok_rows, 1, slice_width),
        "head",
        split_axis=0,
        concat_axis=1,
        tiled=True,
    )
    context_tok = context_back.reshape(tok_rows, D)
    attn = jnp.dot(context_tok, w_out, preferred_element_type=jnp.float32) + biases[2]
    first_sum = tokens.astype(jnp.float32) + attn
    norm_one, first_pull = jax.vjp(layer_norm, first_sum, norm_gains[0], biases[3])
    norm_low = norm_one.astype(jnp.bfloat16)
    hidden_up = jnp.dot(norm_low, w_up, preferred_element_type=jnp.float32) + bias_up
    activated_full, gelu_pull = jax.vjp(exact_gelu, hidden_up)
    activated = activated_full.astype(jnp.bfloat16)
    branch = jnp.dot(activated, w_down, preferred_element_type=jnp.float32) + biases[4]
    out_full, second_pull = jax.vjp(layer_norm, norm_one + branch, norm_gains[1], biases[5])
    leading = out_full.reshape(own_seqs, SLOT, D)[:, 0].astype(jnp.bfloat16)
    pooled = jnp.tanh(jnp.dot(leading, w_pool, preferred_element_type=jnp.float32) + biases[6])
    pooled_low = pooled.astype(jnp.bfloat16)
    logits = against(pooled_low, w_class)
    onehot = (jnp.arange(CLASSES)[None, :] == own_labels[:, None]).astype(jnp.float32)
    losses = jax.nn.logsumexp(logits, axis=-1) - jnp.sum(onehot * logits, axis=-1)
    d_logits = jax.nn.softmax(logits, axis=-1) - onehot
    g_class = exact(d_logits.T, pooled_low.astype(jnp.float32))
    d_pre = exact(d_logits, w_class.astype(jnp.float32)) * (1.0 - pooled * pooled)
    g_pool = exact(leading.astype(jnp.float32).T, d_pre)
    g_pool_bias = jnp.sum(d_pre, axis=0)
    d_leading = exact(d_pre, w_pool.astype(jnp.float32).T)
    d_out = cotangent.astype(jnp.float32) * slot_live[:, None]
    d_out = d_out.reshape(own_seqs, SLOT, D).at[:, 0].add(d_leading).reshape(tok_rows, D)
    d_h2, g_gain_two, g_shift_two = second_pull(d_out)
    d_branch = d_h2.astype(jnp.bfloat16)
    g_bias_down = jnp.sum(d_branch.astype(jnp.float32), axis=0)
    g_down = inner(activated, d_branch)
    d_activated = against(d_branch, w_down)
    d_up = gelu_pull(d_activated)[0].astype(jnp.bfloat16)
    g_bias_up = jnp.sum(d_up.astype(jnp.float32), axis=0)
    g_up = inner(norm_low, d_up)
    d_norm_one = d_h2 + against(d_up, w_up)
    d_h1, g_gain_one, g_shift_one = first_pull(d_norm_one)
    d_attn = d_h1.astype(jnp.bfloat16)
    g_bias_out = jnp.sum(d_attn.astype(jnp.float32), axis=0)
    g_out = inner(context_tok, d_attn)
    d_context = against(d_attn, w_out).astype(jnp.bfloat16)
    d_context_heads = lax.all_to_all(
        d_context.reshape(tok_rows, head_parts, slice_width),
        "head",
        split_axis=1,
        concat_axis=0,
        tiled=True,
    )
    d_context_seq = d_context_heads.reshape(head_parts * own_seqs, SLOT, local_heads, HEAD_DIM)
    d_seq = lax.map(attend_backward, (seq_view, log_total, d_context_seq, lengths))
    d_back = lax.all_to_all(
        d_seq.reshape(head_parts * tok_rows, 3, 1, slice_width),
        "head",
        split_axis=0,
        concat_axis=2,
        tiled=True,
    )
    d_packed = d_back.reshape(tok_rows, 3 * D)
    g_qkv = inner(tokens, d_packed)
    column_sums = jnp.sum(d_packed.astype(jnp.float32), axis=0)
    grad_tokens = (d_h1 + against(d_packed, w_qkv)).astype(jnp.bfloat16)
    g_biases = jnp.stack(
        [column_sums[:D], column_sums[2 * D :], g_bias_out, g_shift_one, g_bias_down, g_shift_two]
    )
    g_gains = jnp.stack([g_gain_one, g_gain_two])
    g_qkv, g_out, g_up, g_down, g_pool, g_class, g_biases, g_gains, g_bias_up, g_pool_bias = (
        lax.psum_scatter(g_qkv, ("batch", "head"), scatter_dimension=1, tiled=True),
        lax.psum_scatter(g_out, ("batch", "head"), scatter_dimension=1, tiled=True),
        lax.psum_scatter(g_up, ("batch", "head"), scatter_dimension=1, tiled=True),
        lax.psum_scatter(g_down, ("batch", "head"), scatter_dimension=1, tiled=True),
        lax.psum_scatter(g_pool, ("batch", "head"), scatter_dimension=1, tiled=True),
        lax.psum_scatter(g_class, ("batch", "head"), scatter_dimension=1, tiled=True),
        lax.psum_scatter(g_biases, ("batch", "head"), scatter_dimension=1, tiled=True),
        lax.psum_scatter(g_gains, ("batch", "head"), scatter_dimension=1, tiled=True),
        lax.psum_scatter(g_bias_up, ("batch", "head"), scatter_dimension=0, tiled=True),
        lax.psum_scatter(g_pool_bias, ("batch", "head"), scatter_dimension=0, tiled=True),
    )
    return (
        out_full.astype(jnp.bfloat16),
        grad_tokens,
        losses,
        g_qkv,
        g_out,
        g_up,
        g_down,
        g_pool,
        g_class,
        g_biases,
        g_gains,
        g_bias_up,
        g_pool_bias,
    )


def solution(mesh):
    return jax.shard_map(
        per_device,
        mesh=mesh,
        in_specs=(
            P(("batch", "head"), None),
            P(("batch", "head"), None),
            P("batch"),
            P("batch"),
            P(),
            P(),
            P(),
            P(),
            P(),
            P(),
            P(),
            P(),
            P(),
        ),
        out_specs=(
            P(("batch", "head"), None),
            P(("batch", "head"), None),
            P(("batch", "head")),
            P(None, ("batch", "head")),
            P(None, ("batch", "head")),
            P(None, ("batch", "head")),
            P(None, ("batch", "head")),
            P(None, ("batch", "head")),
            P(None, ("batch", "head")),
            P(None, ("batch", "head")),
            P(None, ("batch", "head")),
            P(("batch", "head")),
            P(("batch", "head")),
        ),
        check_vma=False,
    )
```

profile of v0, /device:TPU:0, one launch (start us, length us, event | category | flops | bytes accessed | tf_op | source)
XLA Modules:
  0.0 791.8 jit_solution(17786111128805935081)
XLA Ops:
  7.2 1.6 slice_reduce_fusion.1
  9.3 4.5 fusion.34
  13.8 4.3 copy.63
  18.1 3.2 copy.64
  21.3 4.7 all-to-all-start
  26.0 29.1 %all-to-all-done = bf16[512,3,4,192]{0,3,1,2:T(8,128)(2,1)} async-done(((bf16[512,3,4,192]{0,3,1,2:T(8,128)(2,1)}), bf16[512,3,4,192]{0,3,1,2:T(8,128)(2,1)}, u32[]{:S(2)}, u32[]{:S(2)}) %all-to-all-start) | async-done | bytes 2359328 | tf_op jit(solution)/shard_map/all_to_all | solution.py:115
  55.1 24.0 %while.23 = (s32[]{:T(128)}, bf16[4,512,3,64]{1,3,2,0:T(8,128)(2,1)}, f32[4,3,512,1]{2,1,3,0:T(4,128)}, bf16[4,512,3,3,64]{1,4,3,2,0:T(8,128)(2,1)}, s32[4]{0:T(128)S(1)}, /*index=5*/s32[]{:T(128)}) while((s32[]{:T(128)}, bf16[4,512,3,64]{1,3,2,0:T(8,128)(2,1)}, f32[4,3,512,1]{2,1,3,0:T(4,128)}, bf16[4,512,3,3,64]{1,4,3,2,0:T(8,128)(2,1)}, ...), condition=%wide.region_3.4_spmd, body=%wide.region_0.3_spmd.sunk | while | flops 210074624 | bytes 11459673 | solution.py:123
  79.1 2.6 copy.65
  81.8 2.8 reshape.337
  85.1 3.0 reduce.38
  88.1 2.2 copy.87
  90.3 3.9 reshape.384
  94.3 4.2 all-to-all-start.1
  104.6 5.5 all-to-all-done.1
  110.2 4.1 reshape.385
  114.3 5.7 copy.67
  120.1 3.0 all_to_all.48
  124.4 2.7 fusion.56
  128.2 19.6 %multiply_convert_fusion.1 = (bf16[512,3072]{1,0:T(8,128)(2,1)S(1)}, f32[512,3072]{1,0:T(8,128)}, f32[512,3072]{1,0:T(8,128)}) fusion(f32[3072]{0:T(1024)S(1)} %copy-done.37, bf16[768,3072]{1,0:T(8,128)(2,1)} %param.25, f32[512,768]{1,0:T(8,128)S(1)} %get-tuple-element.165, f32[768]{0:T(1024)S(1)} %copy-done.32, f32[768]{0:T(1024)S(1)} %get-tuple-element.176, ...), kind=kOutput, calls=%fused_computation.50 | convolution fusion | flops 2521694208 | bytes 22042624 | tf_op jit(solution)/shard_map/dot_general | solution.py:136
  148.0 2.8 fusion.57
  155.5 2.0 fusion.45
  157.5 1.9 divide_subtract_fusion
  163.2 3.2 multiply_reduce_fusion.1
  167.2 2.1 fusion.53
  169.3 1.7 broadcast_multiply_fusion
  172.7 9.5 %convert_reduce_fusion = (f32[3072]{0:T(1024)}, bf16[512,3072]{1,0:T(8,128)(2,1)S(1)}) fusion(f32[512,3072]{1,0:T(8,128)} %get-tuple-element.156, f32[512,3072]{1,0:T(8,128)} %get-tuple-element.166, f32[3072]{0:T(1024)} %param.31, bf16[512,768]{1,0:T(8,128)(2,1)S(1)} %get-tuple-element.148, bf16[3072,768]{1,0:T(8,128)(2,1)} %param.26), kind=kOutput, calls=%fused_computation.48 | convolution fusion | flops 2442654720 | bytes 21258240 | tf_op jit(solution)/shard_map/dot_general | solution.py:30
  182.2 7.3 multiply_reduce_fusion.2
  192.4 1.7 convolution_convert_fusion
  194.1 2.3 copy.69
  196.5 4.2 all-to-all-start.2
  200.9 3.6 fusion.60
  204.6 7.8 all-to-all-done.2
  212.4 39.9 %while.24 = (s32[]{:T(128)}, bf16[4,512,3,3,64]{1,4,3,2,0:T(8,128)(2,1)}, bf16[4,512,3,3,64]{1,4,3,2,0:T(8,128)(2,1)}, s32[4]{0:T(128)}, f32[4,3,512,1]{2,1,3,0:...) while((s32[]{:T(128)}, bf16[4,512,3,3,64]{1,4,3,2,0:T(8,128)(2,1)}, ...), condition=%wide.region_16.17_spmd, body=%wide.region_14.16_spmd.sunk | while | flops 512654336 | bytes 27953856 | solution.py:177
  252.3 4.9 copy.70
  257.2 5.9 reshape.346
  263.1 7.0 copy.71
  270.0 53.9 %all_to_all.60 = bf16[2048,3,1,192]{3,1,2,0:T(4,128)(2,1)} all-to-all(bf16[2048,3,1,192]{3,1,2,0:T(4,128)(2,1)} %copy.71), channel_id=1, replica_groups=mesh['batch'=8,'head'=4] {'head'}, dimensions={0} | all-to-all | bytes 4718592 | tf_op jit(solution)/shard_map/all_to_all | solution.py:178
  323.9 7.4 copy.80
  331.3 2.2 copy.73
  335.0 5.0 convolution_bitcast_fusion
  340.2 8.8 %fusion.48 = f32[768,3072]{0,1:T(8,128)} fusion(bf16[512,3072]{1,0:T(8,128)(2,1)} %copy-done.43, f32[512,768]{1,0:T(8,128)} %copy-done.6, f32[768]{0:T(1024)} %get-tuple-element.107, f32[768]{0:T(1024)S(1)} %copy-done.27, f32[512]{0:T(512)} %copy-done.28, f32[512]{0:T(512)S(1)} %copy-done.17), kind=kOutput, calls=%fused_computation.138 | convolution fusion | flops 2417885184 | bytes 14166016 | tf_op jit(solution)/shard_map/dot_general | solution.py:24
  349.1 8.4 %fusion.61 = f32[3072,768]{0,1:T(8,128)} fusion(bf16[512,3072]{1,0:T(8,128)(2,1)} %copy-done.42, bf16[512,768]{1,0:T(8,128)(2,1)} %copy-done.13), kind=kOutput, calls=%fused_computation.148 | convolution fusion | flops 2415919104 | bytes 13369344 | tf_op jit(solution)/shard_map/dot_general | solution.py:24
  365.2 2.7 convert_reduce_fusion.1
  375.8 42.2 %all-reduce.5 = (f32[3,768]{1,0:T(4,128)}, f32[6,768]{1,0:T(8,128)}, f32[2,768]{1,0:T(2,128)}, f32[3072]{0:T(1024)}, f32[768]{0:T(1024)}) all-reduce(f32[3,768]{1,0:T(4,128)S(1)} %broadcast_multiply_fusion.1, f32[6,768]{1,0:T(8,128)} %stack.38, ...), channel_id=7, replica_groups=mesh['batch'=8,'head'=4] {'batch','head'}, use_global_device_ids=true, to_apply=%region_24.25.clone | all-reduce | flops 12288 | bytes 98304
  424.6 5.1 add_convert_fusion.1
  429.7 70.9 %reduce-scatter.9.cloned.1.call-done = f32[768,72]{0,1:T(8,128)} async-done(((f32[768,2304]{0,1:T(8,128)}), f32[768,72]{0,1:T(8,128)}) %reduce-scatter.9.cloned.1.call-update) | async-done | bytes 221200 | tf_op jit(solution)/shard_map/reduce_scatter | solution.py:194
  500.6 142.2 %reduce-scatter.13.cloned.1.call-done = f32[768,96]{0,1:T(8,128)} async-done(((f32[768,3072]{0,1:T(8,128)}), f32[768,96]{0,1:T(8,128)}) %reduce-scatter.13.cloned.1.call-update) | async-done | bytes 294928 | tf_op jit(solution)/shard_map/reduce_scatter | solution.py:196
  642.8 140.9 %reduce-scatter.15.cloned.1.call-done = f32[3072,24]{0,1:T(8,128)} async-done(((f32[3072,768]{0,1:T(8,128)}), f32[3072,24]{0,1:T(8,128)}) %reduce-scatter.15.cloned.1.call-update) | async-done | bytes 294928 | tf_op jit(solution)/shard_map/reduce_scatter | solution.py:197
  (238 shorter events, 108.5 us)
Async XLA Ops:
  7.2 2.1 copy-start
  8.8 139.0 %copy-start.26 = (f32[768]{0:T(1024)}, f32[768]{0:T(1024)S(1)}, u32[]{:S(2)}) copy-start(f32[768]{0:T(1024)S(1)} %get-tuple-element.176) | copy-start | bytes 9220
  21.3 33.8 %copy-start.40 = (s32[4]{0:T(128)S(1)}, s32[4]{0:T(128)}, u32[]{:S(2)}) copy-start(s32[4]{0:T(128)} %param.21) | copy-start | bytes 52
  21.3 33.8 %all-to-all-start = ((bf16[512,3,4,192]{0,3,1,2:T(8,128)(2,1)}), bf16[512,3,4,192]{0,3,1,2:T(8,128)(2,1)}, u32[]{:S(2)}, u32[]{:S(2)}) async-start(bf16[512,3,4,192]{0,3,1,2:T(8,128)(2,1)} %copy.64), calls=%async_computation | async-start | bytes 4718592 | tf_op jit(solution)/shard_map/all_to_all | solution.py:115
  85.1 15.2 %copy-start.39 = (s32[4]{0:T(128)S(1)}, s32[4]{0:T(128)}, u32[]{:S(2)}) copy-start(s32[4]{0:T(128)} %param.22) | copy-start | bytes 52
  94.3 15.9 %all-to-all-start.1 = ((bf16[4,2,49152]{2,1,0:T(2,128)(2,1)}), bf16[4,2,49152]{2,1,0:T(2,128)(2,1)}, u32[]{:S(2)}, u32[]{:S(2)}) async-start(bf16[4,2,49152]{2,1,0:T(2,128)(2,1)} %reshape.384), calls=%async_computation.1 | async-start | bytes 1572864 | tf_op jit(solution)/shard_map/all_to_all | solution.py:124
  98.5 331.2 %reduce-scatter.17.cloned.1.call-start = ((), (), s32[]{:S(2)}) async-start(), calls=%async_computation.13 | async-start | bytes 2433024 | tf_op jit(solution)/shard_map/reduce_scatter | solution.py:198
  114.3 10.0 %copy-start.34 = (f32[768]{0:T(1024)S(1)}, f32[768]{0:T(1024)}, u32[]{:S(2)}) copy-start(f32[768]{0:T(1024)} %get-tuple-element.108) | copy-start | bytes 9220
  124.3 3.1 copy-start.11
  124.3 3.9 copy-start.32
  124.3 3.9 copy-start.37
  124.4 23.6 %slice-start = ((s8[4718592]{0:T(1024)(128)(4,1)}), s8[4194304]{0:T(1024)(128)(4,1)S(1)}, s32[]{:S(2)}) async-start(s8[4718592]{0:T(1024)(128)(4,1)} %bitcast.202), calls=%async_computation.14 | async-start | bytes 8388608
  127.1 20.8 %copy-start.6 = (f32[512,768]{1,0:T(8,128)}, f32[512,768]{1,0:T(8,128)S(1)}, u32[]{:S(2)}) copy-start(f32[512,768]{1,0:T(8,128)S(1)} %get-tuple-element.165) | copy-start | bytes 4718596
  127.1 20.8 %copy-start.16 = (f32[512]{0:T(512)}, f32[512]{0:T(512)S(1)}, u32[]{:S(2)}) copy-start(f32[512]{0:T(512)S(1)} %broadcast_multiply_fusion.3) | copy-start | bytes 6148
  128.2 19.7 %copy-start.28 = (f32[512]{0:T(512)}, f32[512]{0:T(512)S(1)}, u32[]{:S(2)}) copy-start(f32[512]{0:T(512)S(1)} %fusion.43) | copy-start | bytes 6148
  128.2 19.7 %copy-start.33 = (f32[768]{0:T(1024)S(1)}, f32[768]{0:T(1024)}, u32[]{:S(2)}) copy-start(f32[768]{0:T(1024)} %get-tuple-element.106) | copy-start | bytes 9220
  128.2 19.7 %slice-start.1 = ((s8[4718592]{0:T(1024)(128)(4,1)}), s8[524288]{0:T(1024)(128)(4,1)S(1)}, s32[]{:S(2)}) async-start(s8[4718592]{0:T(1024)(128)(4,1)} %bitcast.202), calls=%async_computation.15 | async-start | bytes 1048576
  147.9 2.9 copy-start.42
  150.7 10.5 %copy-start.1 = (f32[512,768]{1,0:T(8,128)}, f32[512,768]{1,0:T(8,128)S(1)}, u32[]{:S(2)}) copy-start(f32[512,768]{1,0:T(8,128)S(1)} %get-tuple-element.168) | copy-start | bytes 4718596
  150.8 1.9 copy-start.10
  150.8 2.7 copy-start.38
  150.8 10.5 %copy-start.25 = (f32[768]{0:T(1024)S(1)}, f32[768]{0:T(1024)}, u32[]{:S(2)}) copy-start(f32[768]{0:T(1024)} %slice_reduce_fusion) | copy-start | bytes 9220
  163.2 3.9 copy-start.2
  163.2 3.9 copy-start.4
  166.5 2.8 copy-start.30
  166.5 2.8 copy-start.23
  172.6 9.6 %copy-start.13 = (bf16[512,768]{1,0:T(8,128)(2,1)}, bf16[512,768]{1,0:T(8,128)(2,1)S(1)}, u32[]{:S(2)}) copy-start(bf16[512,768]{1,0:T(8,128)(2,1)S(1)} %get-tuple-element.148) | copy-start | bytes 2359300
  172.6 9.6 %copy-start.7 = (f32[512,768]{1,0:T(8,128)S(1)}, f32[512,768]{1,0:T(8,128)}, u32[]{:S(2)}) copy-start(f32[512,768]{1,0:T(8,128)} %copy-done.6) | copy-start | bytes 4718596
  172.6 9.6 %copy-start.9 = (f32[512,768]{1,0:T(8,128)S(1)}, f32[512,768]{1,0:T(8,128)}, u32[]{:S(2)}) copy-start(f32[512,768]{1,0:T(8,128)} %get-tuple-element.154) | copy-start | bytes 4718596
  172.7 9.6 %copy-start.17 = (f32[512]{0:T(512)S(1)}, f32[512]{0:T(512)}, u32[]{:S(2)}) copy-start(f32[512]{0:T(512)} %copy-done.16) | copy-start | bytes 6148
  172.7 9.5 %copy-start.27 = (f32[768]{0:T(1024)S(1)}, f32[768]{0:T(1024)}, u32[]{:S(2)}) copy-start(f32[768]{0:T(1024)} %copy-done.26) | copy-start | bytes 9220
  172.7 9.5 %copy-start.29 = (f32[512]{0:T(512)S(1)}, f32[512]{0:T(512)}, u32[]{:S(2)}) copy-start(f32[512]{0:T(512)} %copy-done.28) | copy-start | bytes 6148
  182.2 7.3 copy-start.43
  182.2 7.3 copy-start.19
  189.5 2.9 copy-start.36
  196.5 15.9 %all-to-all-start.2 = ((bf16[512,4,192]{0,2,1:T(8,128)(2,1)}), bf16[512,4,192]{0,2,1:T(8,128)(2,1)}, u32[]{:S(2)}, u32[]{:S(2)}) async-start(bf16[512,4,192]{0,2,1:T(8,128)(2,1)} %bitcast.198), calls=%async_computation.2 | async-start | bytes 1572864 | tf_op jit(solution)/shard_map/all_to_all | solution.py:169
  200.7 229.0 %reduce-scatter.11.cloned.1.call-start = ((), (), s32[]{:S(2)}) async-start(), calls=%async_computation.10 | async-start | bytes 2433024 | tf_op jit(solution)/shard_map/reduce_scatter | solution.py:195
  204.6 296.0 %reduce-scatter.9.cloned.1.call-start = ((), (), s32[]{:S(2)}) async-start(), calls=%async_computation.9 | async-start | bytes 7299072 | tf_op jit(solution)/shard_map/reduce_scatter | solution.py:194
  212.4 3.4 copy-start.41
  222.4 3.4 copy-start.41
  232.3 3.4 copy-start.41
  242.4 3.4 copy-start.41
  331.3 3.6 copy-start.14
  339.9 302.9 %reduce-scatter.13.cloned.1.call-start = ((), (), s32[]{:S(2)}) async-start(), calls=%async_computation.11 | async-start | bytes 9732096 | tf_op jit(solution)/shard_map/reduce_scatter | solution.py:196
  349.1 434.6 %reduce-scatter.15.cloned.1.call-start = ((), (), s32[]{:S(2)}) async-start(), calls=%async_computation.12 | async-start | bytes 9732096 | tf_op jit(solution)/shard_map/reduce_scatter | solution.py:197
  357.5 2.5 copy-start.22
  357.5 3.8 copy-start.21
  358.2 17.6 %copy-start.24 = (f32[768]{0:T(1024)S(1)}, f32[768]{0:T(1024)}, u32[]{:S(2)}) copy-start(f32[768]{0:T(1024)} %get-tuple-element.172) | copy-start | bytes 9220
  (9 other events, 11.0 us)
Sparse Core Ops, SparseCore 0:
  171.1 100.1 reduce-scatter.16
  278.1 98.0 reduce-scatter.10
  382.4 118.0 reduce-scatter.8
  507.9 134.8 reduce-scatter.12
  649.1 134.5 reduce-scatter.14
where the time goes:
time: 800 us; the launch traced here: 792 us
  waiting for transfers between devices  397 us (50%)
  matrix products  112 us (14%)
  local copies, waits for them, and re-layouts  111 us (14%)
  blocking collectives  96.1 us (12%)
  other arithmetic  42.7 us (5%)
  between operations  18.5 us (2%)
  starting transfers between devices  14.2 us (2%)
    reduce_scatter x1, waiting for transfers between devices, per_device(): lax.psum_scatter(g_up, ('batch', 'head'), scatter_dimension=1, tiled=True)  142 us
    reduce_scatter x1, waiting for transfers between devices, per_device(): lax.psum_scatter(g_down, ('batch', 'head'), scatter_dimension=1, tiled=True)  141 us
    reduce_scatter x1, waiting for transfers between devices, per_device(): lax.psum_scatter(g_qkv, ('batch', 'head'), scatter_dimension=1, tiled=True)  70.9 us
    all_to_all x1, blocking collectives, per_device(): lax.all_to_all(d_seq.reshape(head_parts * tok_rows, 3, 1, slice_width), '...  53.9 us
    unnamed x1, blocking collectives  42.2 us
    all_to_all x1, waiting for transfers between devices, per_device(): lax.all_to_all(packed_low.reshape(tok_rows, 3, head_parts, slice_width),...  29.1 us
    dot_general x4, matrix products, inner(): lax.dot_general(left, right, (((0,), (0,)), ((), ())), preferred_element_...  25.8 us
    dot_general x5, matrix products, against(): lax.dot_general(left, right, (((1,), (1,)), ((), ())), preferred_element_...  24.3 us
  transfers between devices with their start and end apart: 8, of which 6 were waited for; matrix products, arithmetic and copies ran while one was open for 19% of the time, Pallas kernels for 0%

commit v1 on v0

--- a/solution.py
+++ b/solution.py
@@ -112,13 +112,16 @@
         [biases[0], zeros_key, biases[1]]
     )
     packed_low = packed.astype(jnp.bfloat16)
-    head_view = lax.all_to_all(
-        packed_low.reshape(tok_rows, 3, head_parts, slice_width),
-        "head",
-        split_axis=2,
-        concat_axis=0,
-        tiled=True,
-    )
+    x = packed_low.reshape(tok_rows, 3, head_parts, slice_width)
+    ways, here = (lax.axis_size("head"), lax.axis_index("head"))
+    width = x.shape[2] // ways
+    turned = jnp.roll(x, -here * width, axis=2)
+    got = [lax.slice_in_dim(turned, 0, width, axis=2)]
+    for far in range(1, ways):
+        sent = lax.slice_in_dim(turned, far * width, (far + 1) * width, axis=2)
+        got.append(lax.ppermute(sent, "head", [(d, (d + far) % ways) for d in range(ways)]))
+    line = jnp.concatenate(got[::-1], axis=0)
+    head_view = jnp.roll(line, (here + 1) * got[0].shape[0], axis=0)
     seq_view = head_view.reshape(head_parts * own_seqs, SLOT, 3, local_heads, HEAD_DIM)
     context, log_total = lax.map(attend_forward, (seq_view, lengths))
     context_back = lax.all_to_all(

time: 800 us -> 817 us (1.021)
  local copies, waits for them, and re-layouts: 111 us -> 130 us
    all_to_all x1 -> x0, waiting for transfers between devices: 29.1 us -> none  [per_device(): lax.all_to_all(packed_low.reshape(tok_rows, 3, head_parts, slice_width),...]
    ppermute x0 -> x3, waiting for transfers between devices: none -> 25.6 us  [per_device(): lax.ppermute(sent, 'head', [(d, (d + far) % ways) for d in range(ways)])]
    unnamed x98 -> x109, local copies, waits for them, and re-layouts: 23.3 us -> 31.6 us
  transfers between devices with their start and end apart: 8 -> 10, of which waited for: 6 -> 7; matrix products, arithmetic and copies ran while one was open for 19% -> 19% of each run, Pallas kernels for 0% -> 0%
where the time goes in v1:
time: 817 us; the launch traced here: 806 us
  waiting for transfers between devices  391 us (48%)
  local copies, waits for them, and re-layouts  130 us (16%)
  matrix products  112 us (14%)
  blocking collectives  95.2 us (12%)
  other arithmetic  45.9 us (6%)
  between operations  18.5 us (2%)
  starting transfers between devices  12.5 us (2%)
    reduce_scatter x1, waiting for transfers between devices, per_device(): lax.psum_scatter(g_down, ('batch', 'head'), scatter_dimension=1, tiled=True)  142 us
    reduce_scatter x1, waiting for transfers between devices, per_device(): lax.psum_scatter(g_up, ('batch', 'head'), scatter_dimension=1, tiled=True)  141 us
    reduce_scatter x1, waiting for transfers between devices, per_device(): lax.psum_scatter(g_qkv, ('batch', 'head'), scatter_dimension=1, tiled=True)  69.1 us
    all_to_all x1, blocking collectives, per_device(): lax.all_to_all(d_seq.reshape(head_parts * tok_rows, 3, 1, slice_width), '...  53.9 us
    unnamed x1, blocking collectives  41.4 us
    unnamed x109, local copies, waits for them, and re-layouts  31.6 us
    dot_general x4, matrix products, inner(): lax.dot_general(left, right, (((0,), (0,)), ((), ())), preferred_element_...  25.8 us
    ppermute x3, waiting for transfers between devices, per_device(): lax.ppermute(sent, 'head', [(d, (d + far) % ways) for d in range(ways)])  25.6 us
  transfers between devices with their start and end apart: 10, of which 7 were waited for; matrix products, arithmetic and copies ran while one was open for 19% of the time, Pallas kernels for 0%

profile of v1, /device:TPU:0, one launch (start us, length us, event | category | flops | bytes accessed | tf_op | source)
XLA Modules:
  0.0 806.2 jit_solution(4486795924839683524)
XLA Ops:
  9.3 4.5 fusion.34
  13.9 4.3 copy.63
  18.1 2.5 fusion.35
  23.3 2.4 collective-permute-start
  26.5 13.2 %collective-permute-done = bf16[512,3,1,192]{0,3,2,1:T(8,128)(2,1)} collective-permute-done((bf16[512,3,1,192]{0,3,2,1:T(8,128)(2,1)}, bf16[512,3,1,192]{0,3,2,1:T(8,128)(2,1)}, u32[]{:S(2)}, u32[]{:S(2)}) %collective-permute-start) | collective-permute-done | bytes 589856 | tf_op jit(solution)/shard_map/ppermute | solution.py:122
  40.8 12.4 %collective-permute-done.1 = bf16[512,3,1,192]{0,3,2,1:T(8,128)(2,1)} collective-permute-done((bf16[512,3,1,192]{0,3,2,1:T(8,128)(2,1)}, bf16[512,3,1,192]{0,3,2,1:T(8,128)(2,1)}, u32[]{:S(2)}, u32[]{:S(2)}) %collective-permute-start.1) | collective-permute-done | bytes 589856 | tf_op jit(solution)/shard_map/ppermute | solution.py:122
  60.6 6.2 reshape.335
  66.8 3.6 copy.64
  70.4 24.0 %while.23 = (s32[]{:T(128)}, bf16[4,512,3,64]{1,3,2,0:T(8,128)(2,1)}, f32[4,3,512,1]{2,1,3,0:T(4,128)}, bf16[4,512,3,3,64]{1,4,3,2,0:T(8,128)(2,1)}, s32[4]{0:T(128)S(1)}, /*index=5*/s32[]{:T(128)}) while((s32[]{:T(128)}, bf16[4,512,3,64]{1,3,2,0:T(8,128)(2,1)}, f32[4,3,512,1]{2,1,3,0:T(4,128)}, bf16[4,512,3,3,64]{1,4,3,2,0:T(8,128)(2,1)}, ...), condition=%wide.region_3.4_spmd, body=%wide.region_0.3_spmd.sunk | while | flops 210074624 | bytes 11459673 | solution.py:126
  94.4 2.6 copy.65
  97.0 2.8 reshape.336
  100.3 3.0 reduce.38
  103.3 2.2 copy.88
  105.6 3.9 reshape.383
  109.5 4.2 all-to-all-start
  119.5 5.9 all-to-all-done
  125.4 4.1 reshape.384
  129.6 5.7 copy.67
  135.3 3.0 all_to_all.34
  139.6 2.7 fusion.58
  143.5 19.7 %multiply_convert_fusion.1 = (bf16[512,3072]{1,0:T(8,128)(2,1)S(1)}, f32[512,3072]{1,0:T(8,128)}, f32[512,3072]{1,0:T(8,128)}) fusion(f32[3072]{0:T(1024)S(1)} %copy-done.39, bf16[768,3072]{1,0:T(8,128)(2,1)} %param.25, f32[512,768]{1,0:T(8,128)S(1)} %get-tuple-element.190, f32[768]{0:T(1024)S(1)} %copy-done.34, f32[768]{0:T(1024)S(1)} %get-tuple-element.201, ...), kind=kOutput, calls=%fused_computation.50 | convolution fusion | flops 2521694208 | bytes 22042624 | tf_op jit(solution)/shard_map/dot_general | solution.py:139
  163.2 2.8 fusion.59
  170.8 2.0 fusion.46
  172.8 1.9 divide_subtract_fusion
  178.5 3.2 multiply_reduce_fusion.1
  182.5 2.1 fusion.54
  188.0 9.5 %convert_reduce_fusion = (f32[3072]{0:T(1024)}, bf16[512,3072]{1,0:T(8,128)(2,1)S(1)}) fusion(f32[512,3072]{1,0:T(8,128)} %get-tuple-element.178, f32[512,3072]{1,0:T(8,128)} %get-tuple-element.191, f32[3072]{0:T(1024)} %param.31, bf16[512,768]{1,0:T(8,128)(2,1)S(1)} %get-tuple-element.170, bf16[3072,768]{1,0:T(8,128)(2,1)} %param.26), kind=kOutput, calls=%fused_computation.48 | convolution fusion | flops 2442654720 | bytes 21258240 | tf_op jit(solution)/shard_map/dot_general | solution.py:30
  197.6 7.3 multiply_reduce_fusion.2
  209.5 2.3 copy.69
  211.8 4.2 all-to-all-start.1
  216.5 3.6 fusion.62
  220.1 7.6 all-to-all-done.1
  227.7 39.8 %while.24 = (s32[]{:T(128)}, bf16[4,512,3,3,64]{1,4,3,2,0:T(8,128)(2,1)}, bf16[4,512,3,3,64]{1,4,3,2,0:T(8,128)(2,1)}, s32[4]{0:T(128)}, f32[4,3,512,1]{2,1,3,0:...) while((s32[]{:T(128)}, bf16[4,512,3,3,64]{1,4,3,2,0:T(8,128)(2,1)}, ...), condition=%wide.region_16.17_spmd, body=%wide.region_14.16_spmd.sunk | while | flops 512654336 | bytes 27953856 | solution.py:180
  267.6 4.9 copy.71
  272.5 5.9 reshape.345
  278.3 6.9 copy.72
  285.3 53.9 %all_to_all.45 = bf16[2048,3,1,192]{3,1,2,0:T(4,128)(2,1)} all-to-all(bf16[2048,3,1,192]{3,1,2,0:T(4,128)(2,1)} %copy.72), channel_id=1, replica_groups=mesh['batch'=8,'head'=4] {'head'}, dimensions={0} | all-to-all | bytes 4718592 | tf_op jit(solution)/shard_map/all_to_all | solution.py:181
  339.1 7.6 copy.81
  346.7 2.2 copy.74
  350.3 5.0 convolution_bitcast_fusion
  355.5 8.4 %fusion.63 = f32[3072,768]{0,1:T(8,128)} fusion(bf16[512,3072]{1,0:T(8,128)(2,1)} %copy-done.44, bf16[512,768]{1,0:T(8,128)(2,1)} %copy-done.15), kind=kOutput, calls=%fused_computation.161 | convolution fusion | flops 2415919104 | bytes 13369344 | tf_op jit(solution)/shard_map/dot_general | solution.py:24
  364.0 8.8 %fusion.49 = f32[768,3072]{0,1:T(8,128)} fusion(bf16[512,3072]{1,0:T(8,128)(2,1)} %copy-done.45, f32[512,768]{1,0:T(8,128)} %copy-done.8, f32[768]{0:T(1024)} %get-tuple-element.129, f32[768]{0:T(1024)S(1)} %copy-done.29, f32[512]{0:T(512)} %copy-done.30, f32[512]{0:T(512)S(1)} %copy-done.19), kind=kOutput, calls=%fused_computation.150 | convolution fusion | flops 2417885184 | bytes 14166016 | tf_op jit(solution)/shard_map/dot_general | solution.py:24
  382.5 2.7 convert_reduce_fusion.1
  393.1 41.4 %all-reduce.5 = (f32[3,768]{1,0:T(4,128)}, f32[6,768]{1,0:T(8,128)}, f32[2,768]{1,0:T(2,128)}, f32[3072]{0:T(1024)}, f32[768]{0:T(1024)}) all-reduce(f32[3,768]{1,0:T(4,128)S(1)} %broadcast_multiply_fusion.1, f32[6,768]{1,0:T(8,128)} %stack.38, ...), channel_id=7, replica_groups=mesh['batch'=8,'head'=4] {'batch','head'}, use_global_device_ids=true, to_apply=%region_24.25.clone | all-reduce | flops 12288 | bytes 98304
  441.0 5.1 add_convert_fusion.1
  446.1 69.1 %reduce-scatter.9.cloned.1.call-done = f32[768,72]{0,1:T(8,128)} async-done(((f32[768,2304]{0,1:T(8,128)}), f32[768,72]{0,1:T(8,128)}) %reduce-scatter.9.cloned.1.call-update) | async-done | bytes 221200 | tf_op jit(solution)/shard_map/reduce_scatter | solution.py:197
  515.2 142.3 %reduce-scatter.15.cloned.1.call-done = f32[3072,24]{0,1:T(8,128)} async-done(((f32[3072,768]{0,1:T(8,128)}), f32[3072,24]{0,1:T(8,128)}) %reduce-scatter.15.cloned.1.call-update) | async-done | bytes 294928 | tf_op jit(solution)/shard_map/reduce_scatter | solution.py:200
  657.5 140.8 %reduce-scatter.13.cloned.1.call-done = f32[768,96]{0,1:T(8,128)} async-done(((f32[768,3072]{0,1:T(8,128)}), f32[768,96]{0,1:T(8,128)}) %reduce-scatter.13.cloned.1.call-update) | async-done | bytes 294928 | tf_op jit(solution)/shard_map/reduce_scatter | solution.py:199
  (258 shorter events, 126.9 us)
Async XLA Ops:
  8.9 154.3 %copy-start.28 = (f32[768]{0:T(1024)}, f32[768]{0:T(1024)S(1)}, u32[]{:S(2)}) copy-start(f32[768]{0:T(1024)S(1)} %get-tuple-element.201) | copy-start | bytes 9220
  23.3 16.4 %collective-permute-start = (bf16[512,3,1,192]{0,3,2,1:T(8,128)(2,1)}, bf16[512,3,1,192]{0,3,2,1:T(8,128)(2,1)}, u32[]{:S(2)}, u32[]{:S(2)}) collective-permute-start(bf16[512,3,1,192]{0,3,2,1:T(8,128)(2,1)} %get-tuple-element.185), channel_id=1, source_target_pairs={{0,3},{1,0},{2,1},{3,2},{4,7},{5,4},{6,5},{7,6},{8,11},{9,8},{10,9... | collective-permute-start | bytes 1769480 | tf_op jit(solution)/shard_map/ppermute | solution.py:122
  25.7 27.5 %collective-permute-start.1 = (bf16[512,3,1,192]{0,3,2,1:T(8,128)(2,1)}, bf16[512,3,1,192]{0,3,2,1:T(8,128)(2,1)}, u32[]{:S(2)}, u32[]{:S(2)}) collective-permute-start(bf16[512,3,1,192]{0,3,2,1:T(8,128)(2,1)} %get-tuple-element.184), channel_id=1, source_target_pairs={{0,2},{1,3},{2,0},{3,1},{4,6},{5,7},{6,4},{7,5},{8,10},{9,11},{10,... | collective-permute-start | bytes 1769480 | tf_op jit(solution)/shard_map/ppermute | solution.py:122
  26.2 28.1 %collective-permute-start.2 = (bf16[512,3,1,192]{0,3,2,1:T(8,128)(2,1)}, bf16[512,3,1,192]{0,3,2,1:T(8,128)(2,1)}, u32[]{:S(2)}, u32[]{:S(2)}) collective-permute-start(bf16[512,3,1,192]{0,3,2,1:T(8,128)(2,1)} %get-tuple-element.183), channel_id=1, source_target_pairs={{0,1},{1,2},{2,3},{3,0},{4,5},{5,6},{6,7},{7,4},{8,9},{9,10},{10,1... | collective-permute-start | bytes 1769480 | tf_op jit(solution)/shard_map/ppermute | solution.py:122
  26.4 29.0 %copy-start.6 = (bf16[512,3,4,192]{0,3,2,1:T(8,128)(2,1)S(1)}, bf16[512,3,4,192]{0,3,2,1:T(8,128)(2,1)}, u32[]{:S(2)}) copy-start(bf16[512,3,4,192]{0,3,2,1:T(8,128)(2,1)} %copy-done.5) | copy-start | bytes 7077892
  66.8 3.6 copy-start.42
  100.3 14.9 %copy-start.41 = (s32[4]{0:T(128)S(1)}, s32[4]{0:T(128)}, u32[]{:S(2)}) copy-start(s32[4]{0:T(128)} %param.22) | copy-start | bytes 52
  109.5 15.9 %all-to-all-start = ((bf16[4,2,49152]{2,1,0:T(2,128)(2,1)}), bf16[4,2,49152]{2,1,0:T(2,128)(2,1)}, u32[]{:S(2)}, u32[]{:S(2)}) async-start(bf16[4,2,49152]{2,1,0:T(2,128)(2,1)} %reshape.383), calls=%async_computation | async-start | bytes 1572864 | tf_op jit(solution)/shard_map/all_to_all | solution.py:127
  113.7 332.4 %reduce-scatter.17.cloned.1.call-start = ((), (), s32[]{:S(2)}) async-start(), calls=%async_computation.12 | async-start | bytes 2433024 | tf_op jit(solution)/shard_map/reduce_scatter | solution.py:201
  129.6 10.0 %copy-start.36 = (f32[768]{0:T(1024)S(1)}, f32[768]{0:T(1024)}, u32[]{:S(2)}) copy-start(f32[768]{0:T(1024)} %get-tuple-element.130) | copy-start | bytes 9220
  139.6 3.1 copy-start.13
  139.6 3.9 copy-start.34
  139.6 3.9 copy-start.39
  139.6 23.6 %slice-start = ((s8[4718592]{0:T(1024)(128)(4,1)}), s8[4194304]{0:T(1024)(128)(4,1)S(1)}, s32[]{:S(2)}) async-start(s8[4718592]{0:T(1024)(128)(4,1)} %bitcast.201), calls=%async_computation.13 | async-start | bytes 8388608
  142.3 20.8 %copy-start.8 = (f32[512,768]{1,0:T(8,128)}, f32[512,768]{1,0:T(8,128)S(1)}, u32[]{:S(2)}) copy-start(f32[512,768]{1,0:T(8,128)S(1)} %get-tuple-element.190) | copy-start | bytes 4718596
  142.3 20.8 %copy-start.18 = (f32[512]{0:T(512)}, f32[512]{0:T(512)S(1)}, u32[]{:S(2)}) copy-start(f32[512]{0:T(512)S(1)} %broadcast_multiply_fusion.3) | copy-start | bytes 6148
  143.4 19.8 %copy-start.30 = (f32[512]{0:T(512)}, f32[512]{0:T(512)S(1)}, u32[]{:S(2)}) copy-start(f32[512]{0:T(512)S(1)} %fusion.44) | copy-start | bytes 6148
  143.4 19.8 %copy-start.35 = (f32[768]{0:T(1024)S(1)}, f32[768]{0:T(1024)}, u32[]{:S(2)}) copy-start(f32[768]{0:T(1024)} %get-tuple-element.128) | copy-start | bytes 9220
  143.4 19.8 %slice-start.1 = ((s8[4718592]{0:T(1024)(128)(4,1)}), s8[524288]{0:T(1024)(128)(4,1)S(1)}, s32[]{:S(2)}) async-start(s8[4718592]{0:T(1024)(128)(4,1)} %bitcast.201), calls=%async_computation.14 | async-start | bytes 1048576
  163.2 2.9 copy-start.44
  166.0 10.5 %copy-start.1 = (f32[512,768]{1,0:T(8,128)}, f32[512,768]{1,0:T(8,128)S(1)}, u32[]{:S(2)}) copy-start(f32[512,768]{1,0:T(8,128)S(1)} %get-tuple-element.193) | copy-start | bytes 4718596
  166.1 2.7 copy-start.40
  166.1 10.5 %copy-start.27 = (f32[768]{0:T(1024)S(1)}, f32[768]{0:T(1024)}, u32[]{:S(2)}) copy-start(f32[768]{0:T(1024)} %slice_reduce_fusion) | copy-start | bytes 9220
  178.5 3.9 copy-start.2
  178.5 3.9 copy-start.4
  181.8 2.8 copy-start.32
  181.8 2.8 copy-start.25
  187.9 9.6 %copy-start.15 = (bf16[512,768]{1,0:T(8,128)(2,1)}, bf16[512,768]{1,0:T(8,128)(2,1)S(1)}, u32[]{:S(2)}) copy-start(bf16[512,768]{1,0:T(8,128)(2,1)S(1)} %get-tuple-element.170) | copy-start | bytes 2359300
  187.9 9.6 %copy-start.9 = (f32[512,768]{1,0:T(8,128)S(1)}, f32[512,768]{1,0:T(8,128)}, u32[]{:S(2)}) copy-start(f32[512,768]{1,0:T(8,128)} %copy-done.8) | copy-start | bytes 4718596
  187.9 9.6 %copy-start.11 = (f32[512,768]{1,0:T(8,128)S(1)}, f32[512,768]{1,0:T(8,128)}, u32[]{:S(2)}) copy-start(f32[512,768]{1,0:T(8,128)} %get-tuple-element.176) | copy-start | bytes 4718596
  187.9 9.6 %copy-start.19 = (f32[512]{0:T(512)S(1)}, f32[512]{0:T(512)}, u32[]{:S(2)}) copy-start(f32[512]{0:T(512)} %copy-done.18) | copy-start | bytes 6148
  188.0 9.6 %copy-start.29 = (f32[768]{0:T(1024)S(1)}, f32[768]{0:T(1024)}, u32[]{:S(2)}) copy-start(f32[768]{0:T(1024)} %copy-done.28) | copy-start | bytes 9220
  188.0 9.6 %copy-start.31 = (f32[512]{0:T(512)S(1)}, f32[512]{0:T(512)}, u32[]{:S(2)}) copy-start(f32[512]{0:T(512)} %copy-done.30) | copy-start | bytes 6148
  197.5 7.3 copy-start.45
  197.6 7.3 copy-start.21
  204.8 2.9 copy-start.38
  211.8 15.9 %all-to-all-start.1 = ((bf16[512,4,192]{0,2,1:T(8,128)(2,1)}), bf16[512,4,192]{0,2,1:T(8,128)(2,1)}, u32[]{:S(2)}, u32[]{:S(2)}) async-start(bf16[512,4,192]{0,2,1:T(8,128)(2,1)} %bitcast.197), calls=%async_computation.1 | async-start | bytes 1572864 | tf_op jit(solution)/shard_map/all_to_all | solution.py:172
  216.0 230.1 %reduce-scatter.11.cloned.1.call-start = ((), (), s32[]{:S(2)}) async-start(), calls=%async_computation.9 | async-start | bytes 2433024 | tf_op jit(solution)/shard_map/reduce_scatter | solution.py:198
  220.1 295.1 %reduce-scatter.9.cloned.1.call-start = ((), (), s32[]{:S(2)}) async-start(), calls=%async_computation.8 | async-start | bytes 7299072 | tf_op jit(solution)/shard_map/reduce_scatter | solution.py:197
  227.7 3.4 copy-start.43
  237.7 3.4 copy-start.43
  247.7 3.4 copy-start.43
  257.6 3.4 copy-start.43
  346.7 3.6 copy-start.16
  355.3 302.2 %reduce-scatter.15.cloned.1.call-start = ((), (), s32[]{:S(2)}) async-start(), calls=%async_computation.11 | async-start | bytes 9732096 | tf_op jit(solution)/shard_map/reduce_scatter | solution.py:200
  363.9 434.4 %reduce-scatter.13.cloned.1.call-start = ((), (), s32[]{:S(2)}) async-start(), calls=%async_computation.10 | async-start | bytes 9732096 | tf_op jit(solution)/shard_map/reduce_scatter | solution.py:199
  372.8 4.3 copy-start.23
  375.3 17.8 %copy-start.26 = (f32[768]{0:T(1024)S(1)}, f32[768]{0:T(1024)}, u32[]{:S(2)}) copy-start(f32[768]{0:T(1024)} %get-tuple-element.197) | copy-start | bytes 9220
  (13 other events, 17.7 us)
Sparse Core Ops, SparseCore 0:
  186.4 99.4 reduce-scatter.16
  292.6 97.9 reduce-scatter.10
  396.9 118.2 reduce-scatter.8
  522.5 134.9 reduce-scatter.14
  663.9 134.4 reduce-scatter.12
